TPU v7x, 32 devices: a whole 2x2x4 slice. The times are simulated.
32 devices in a mesh: group: 4 (over z), expert: 8 (over y, x, core).
Axes of the slice: x: 2, y: 2, z: 4, core: 2. Of those that a mesh axis runs over, the one named last changes fastest.
Arguments:
- group_logits: float32 [4096, 4], P(('group', 'expert')), may hold values from -6 to 6
- expert_logits: float32 [4096, 32], P(('group', 'expert')), may hold values from -6 to 6
- expert_ids: int32 [4096, 2], P(('group', 'expert')), may hold values from 0 to 31, all different within a row; in each aligned block of 128 rows (0 to 127, 128 to 255, ...) at most 16 rows name the same one
- cotangent: bfloat16 [4096, 3584], P(('group', 'expert')), may hold values from -6 to 6
- hidden_saved: bfloat16 [32, 512, 1024], P(('group', 'expert')), may hold values from -0.1875 to 0.1875
- w_down: bfloat16 [32, 1024, 3584], P(('group', 'expert')), may hold values from -0.1875 to 0.1875
Outputs:
- hidden_grad: bfloat16 [32, 512, 1024], P(('group', 'expert'))
- d_group_logits: float32 [4096, 4], P(('group', 'expert'))
- d_expert_logits: float32 [4096, 32], P(('group', 'expert'))
Inputs may be any that keep to these rules, and one draw needn't show every extreme that they name: `expert_ids`: within the 128 tokens of one device no expert is named by more than 16 choices, a bound that some block reaches; the 2 experts of a token differ.
All inputs are finite; a program needn't handle non-finite values.
Results may differ from a plain program's by a relative error of at most 0.0045.
Values may be sent and summed in bfloat16 or wider, within the bound.
No kernel may reach another device: no remote copies, remote signals or barrier semaphores. Data moves between devices by JAX's collectives and lax.ppermute only.
A program may use at most 64 MiB of HBM per device.

v0:
```python
from functools import partial

import jax
import jax.numpy as jnp
from jax import lax
from jax.experimental import pallas as pl
from jax.experimental.pallas import tpu as pltpu
from jax.sharding import Mesh
from jax.sharding import PartitionSpec as P

ITERS = 5
SOFTCAP = 4.0
LANES = 128
SUBLANES = 8
AXES = ("half", "plane", "expert")
NEAR = ("plane", "expert")
REPLICATED_BYTES = 1 << 20
OWN_VMEM = 24 << 20
OTHER_VMEM = 58880 << 10


def capped(logits):
    return jnp.exp(SOFTCAP * jnp.tanh(logits / SOFTCAP))


def squashing(logits):
    bounded = jnp.tanh(logits / SOFTCAP)
    return 1.0 - bounded * bounded


def balance_level(level_in, target, column_sum):
    scaled = level_in * (target / column_sum)
    return (scaled, jnp.sum(scaled, -1, keepdims=True))


def adjoint_local(out_grad, level_in, target, column_sum):
    scaled, row_total = balance_level(level_in, target, column_sum)
    level_out = scaled / row_total
    scaled_grad = (out_grad - jnp.sum(out_grad * level_out, -1, keepdims=True)) / row_total
    return (scaled_grad, jnp.sum(scaled_grad * level_in, 0))


def adjoint_finish(scaled_grad, inner, target, column_sum):
    return target / column_sum * (scaled_grad - inner / column_sum)


def balance_step(targets, current, unused):
    target_group, target_expert = targets
    group_in, expert_in = current
    group_cols, expert_cols = lax.psum((jnp.sum(group_in, 0), jnp.sum(expert_in, 0)), AXES)
    scaled_g, rowsum_g = balance_level(group_in, target_group, group_cols)
    scaled_e, rowsum_e = balance_level(expert_in, target_expert, expert_cols)
    return (
        (scaled_g / rowsum_g, scaled_e / rowsum_e),
        (group_in, expert_in, group_cols, expert_cols),
    )


def adjoint_step(targets, carried, stored_step):
    target_group, target_expert = targets
    grad_g, grad_e = carried
    group_in, expert_in, group_cols, expert_cols = stored_step
    scaled_g, inner_g = adjoint_local(grad_g, group_in, target_group, group_cols)
    scaled_e, inner_e = adjoint_local(grad_e, expert_in, target_expert, expert_cols)
    inner_g, inner_e = lax.psum((inner_g, inner_e), AXES)
    next_g = adjoint_finish(scaled_g, inner_g, target_group, group_cols)
    next_e = adjoint_finish(scaled_e, inner_e, target_expert, expert_cols)
    return ((next_g, next_e), None)


def slots_of(expert_ids, experts, capacity):
    flat_ids = expert_ids.reshape(-1)
    picked = (flat_ids[:, None] == jnp.arange(experts, dtype=jnp.int32)[None, :]).astype(jnp.int32)
    positions = jnp.sum((jnp.cumsum(picked, 0) - picked) * picked, 1)
    return flat_ids * capacity + positions


def distributed(group_logits, expert_logits, expert_ids, cotangent, hidden_saved, w_down):
    groups = lax.axis_size(("half", "plane"))
    per_group = lax.axis_size("expert")
    experts = groups * per_group
    tokens_here, top_count = expert_ids.shape
    capacity = hidden_saved.shape[1] // experts
    slots = experts * capacity
    targets = (float(tokens_here * per_group), float(tokens_here * groups))
    slot_index = slots_of(expert_ids, experts, capacity)
    serial = jnp.arange(slot_index.shape[0], dtype=jnp.int32)
    source_index = jnp.zeros((slots,), jnp.int32).at[slot_index].set(serial)
    filled = jnp.zeros((slots,), jnp.int32).at[slot_index].set(1)
    fetched = jnp.take(cotangent, source_index // top_count, axis=0)
    send_rows = jnp.where(filled[:, None] > 0, fetched, jnp.zeros_like(fetched))
    expert_rows = lax.all_to_all(send_rows, AXES, split_axis=0, concat_axis=0, tiled=True)
    group_of = expert_ids // per_group
    group_aff = capped(group_logits)
    expert_aff = capped(expert_logits).reshape(tokens_here, groups, per_group)
    (group_prob, expert_prob), stored = lax.scan(
        partial(balance_step, targets), (group_aff, expert_aff), None, length=ITERS
    )
    pick_group = jnp.take_along_axis(group_prob, group_of, 1)
    pick_expert = jnp.take_along_axis(expert_prob.reshape(tokens_here, experts), expert_ids, 1)
    pair_prob = pick_group * pick_expert
    total_prob = jnp.sum(pair_prob, 1, keepdims=True)
    gate_prob = pair_prob / total_prob
    gate_sent = (
        jnp.zeros((slots,), jnp.bfloat16)
        .at[slot_index]
        .set(gate_prob.astype(jnp.bfloat16).reshape(-1))
    )
    got_gates = lax.all_to_all(gate_sent, AXES, split_axis=0, concat_axis=0, tiled=True)
    unscaled = lax.dot_general(
        expert_rows, w_down[0], (((1,), (1,)), ((), ())), preferred_element_type=jnp.float32
    )
    slot_grad = jnp.sum(unscaled * hidden_saved[0].astype(jnp.float32), 1)
    grad_rows = (got_gates.reshape(-1, 1).astype(jnp.float32) * unscaled).astype(jnp.bfloat16)
    answers = lax.all_to_all(slot_grad, AXES, split_axis=0, concat_axis=0, tiled=True)
    gate_grad = answers[slot_index].reshape(tokens_here, top_count)
    pair_grad = (gate_grad - jnp.sum(gate_prob * gate_grad, 1, keepdims=True)) / total_prob
    group_pick = (
        group_of[:, :, None] == jnp.arange(groups, dtype=jnp.int32)[None, None, :]
    ).astype(jnp.float32)
    seed_group = jnp.sum(group_pick * (pair_grad * pick_expert)[:, :, None], 1)
    expert_pick = (
        expert_ids[:, :, None] == jnp.arange(experts, dtype=jnp.int32)[None, None, :]
    ).astype(jnp.float32)
    seed_expert = jnp.sum(expert_pick * (pair_grad * pick_group)[:, :, None], 1).reshape(
        tokens_here, groups, per_group
    )
    (grad_group, grad_expert), unused = lax.scan(
        partial(adjoint_step, targets), (seed_group, seed_expert), stored, reverse=True
    )
    d_group_logits = grad_group * group_aff * squashing(group_logits)
    d_expert_logits = (grad_expert * expert_aff).reshape(tokens_here, experts) * squashing(
        expert_logits
    )
    return (grad_rows[None], d_group_logits, d_expert_logits)


def place_rows(ids, first, experts, capacity):
    lanes = ids[0].shape[1]
    expert = lax.broadcasted_iota(jnp.int32, (experts, lanes), 0)
    hits = [(row - first) == expert for row in ids]
    picked = sum(hit.astype(jnp.float32) for hit in hits)
    earlier = (
        lax.broadcasted_iota(jnp.int32, (lanes, lanes), 0)
        < lax.broadcasted_iota(jnp.int32, (lanes, lanes), 1)
    ).astype(jnp.bfloat16)
    before = jnp.dot(picked.astype(jnp.bfloat16), earlier, preferred_element_type=jnp.float32)
    slot_of = (expert * capacity).astype(jnp.float32) + before
    slot_at = lax.broadcasted_iota(jnp.int32, (experts * capacity, lanes), 0)
    place = jnp.zeros((experts * capacity, lanes), jnp.float32)
    for row, hit in zip(ids, hits):
        slot = jnp.sum(jnp.where(hit, slot_of, 0.0), 0, keepdims=True).astype(jnp.int32)
        here = (row >= first) & (row < first + experts)
        slot = jnp.where(here, slot, -1)
        place = place + (slot == slot_at).astype(jnp.float32)
    return place.astype(jnp.bfloat16)


def row_copies(source, rows_ref, in_sem, packed_ref, out_ref, out_sem, pieces):
    width = out_ref.shape[1] // pieces
    incoming, outgoing = [], []
    for c in range(pieces):
        at = pl.ds(c * width, width)
        incoming.append(
            pltpu.make_async_copy(source.at[:, at], rows_ref.at[:, at], in_sem.at[c])
        )
        outgoing.append(
            pltpu.make_async_copy(packed_ref.at[:, at], out_ref.at[:, at], out_sem.at[c])
        )
    return incoming, outgoing


def pack_pieces(place, rows_ref, packed_ref, incoming, outgoing, cuts=()):
    width = packed_ref.shape[1] // len(incoming)
    for c, copy in enumerate(incoming):
        at = pl.ds(c * width, width)
        copy.wait()
        packed_ref[:, at] = jnp.dot(
            place, rows_ref[:, at], preferred_element_type=jnp.float32
        ).astype(packed_ref.dtype)
        outgoing[c].start()
        if cuts and (c + 1) * len(cuts) % len(incoming) == 0:
            cuts[(c + 1) * len(cuts) // len(incoming) - 1].start()
    for copy in [*outgoing, *cuts]:
        copy.wait()


def first_kernel(
    group_ref, ids_ref, expert_ref, cotangent_ref, mine_ref, out_ref, *refs, near, capacity,
    pieces, parts
):
    blocks, refs = refs[:parts], refs[parts:]
    *small_refs, small_sem, block_sem, rows_ref, packed_ref, in_sem, out_sem = refs
    small = [
        pltpu.make_async_copy(source, target, small_sem.at[i])
        for i, (source, target) in enumerate(zip((group_ref, ids_ref, expert_ref), small_refs))
    ]
    incoming, outgoing = row_copies(
        cotangent_ref, rows_ref, in_sem, packed_ref, out_ref, out_sem, pieces
    )
    part = rows_ref.shape[1] // parts
    cuts = [
        pltpu.make_async_copy(
            rows_ref.at[:, pl.ds(i * part, part)], block, block_sem.at[i]
        )
        for i, block in enumerate(blocks)
    ]
    for copy in small + incoming:
        copy.start()
    for copy in small:
        copy.wait()
    group_on, ids_on, expert_on = small_refs
    groups, top_count = group_on.shape[0], ids_on.shape[0]
    mine_ref[:SUBLANES, :] = jnp.zeros((SUBLANES, mine_ref.shape[1]), jnp.float32)
    mine_ref[:groups, :] = group_on[...]
    mine_ref[groups : groups + top_count, :] = ids_on[...].astype(jnp.float32)
    mine_ref[SUBLANES:, :] = expert_on[...]
    ids = [ids_on[k : k + 1, :] for k in range(top_count)]
    place = place_rows(ids, lax.axis_index("half") * near, near, capacity)
    pack_pieces(place, rows_ref, packed_ref, incoming, outgoing, cuts)


def first_rows(group_logits, expert_ids, expert_logits, cotangent, near, capacity, parts):
    width, dtype = cotangent.shape[1], cotangent.dtype
    slots = near * capacity
    pieces = max(n for n in range(parts, SUBLANES, parts) if width % (n * LANES) == 0)
    small = [group_logits.T, expert_ids.T, expert_logits.T]
    experts, tokens = small[2].shape
    anywhere = pl.BlockSpec(memory_space=pl.ANY)
    return pl.pallas_call(
        partial(first_kernel, near=near, capacity=capacity, pieces=pieces, parts=parts),
        out_shape=[
            jax.ShapeDtypeStruct((SUBLANES + experts, tokens), jnp.float32),
            jax.ShapeDtypeStruct((slots, width), dtype),
        ]
        + [jax.ShapeDtypeStruct((tokens, width // parts), dtype)] * parts,
        in_specs=[anywhere] * 4,
        out_specs=[pl.BlockSpec(memory_space=pltpu.VMEM)] + [anywhere] * (1 + parts),
        scratch_shapes=[pltpu.VMEM(x.shape, x.dtype) for x in small]
        + [pltpu.SemaphoreType.DMA((len(small),)), pltpu.SemaphoreType.DMA((parts,))]
        + [
            pltpu.VMEM((tokens, width), dtype),
            pltpu.VMEM((slots, width), dtype),
            pltpu.SemaphoreType.DMA((pieces,)),
            pltpu.SemaphoreType.DMA((pieces,)),
        ],
        cost_estimate=pl.CostEstimate(
            flops=2 * tokens * slots * width,
            bytes_accessed=2 * width * (tokens + slots),
            transcendentals=0,
        ),
        name="first_rows",
    )(*small, cotangent)


def pack_kernel(small_ref, *refs, near, capacity, first_id, top_count):
    *rows_refs, out_ref, place_ref = refs

    @pl.when(pl.program_id(0) == 0)
    def _():
        ids = [
            small_ref[first_id + k : first_id + k + 1, :].astype(jnp.int32)
            for k in range(top_count)
        ]
        place_ref[...] = place_rows(ids, lax.axis_index("half") * near, near, capacity)

    rows = rows_refs[0][...]
    for rows_ref in rows_refs[1:]:
        rows = rows + rows_ref[...]
    out_ref[...] = jnp.dot(
        place_ref[...], rows, preferred_element_type=jnp.float32
    ).astype(out_ref.dtype)


def pack_rows(small, rows, near, capacity, first_id, top_count):
    tokens, width = rows[0].shape
    dtype = rows[0].dtype
    slots = near * capacity
    block = max(n for n in range(LANES, 8 * LANES, LANES) if width % n == 0)
    return pl.pallas_call(
        partial(
            pack_kernel, near=near, capacity=capacity, first_id=first_id, top_count=top_count
        ),
        out_shape=jax.ShapeDtypeStruct((slots, width), dtype),
        grid=(width // block,),
        in_specs=[pl.BlockSpec(small.shape, lambda i: (0, 0))]
        + [pl.BlockSpec((tokens, block), lambda i: (0, i))] * len(rows),
        out_specs=pl.BlockSpec((slots, block), lambda i: (0, i)),
        scratch_shapes=[pltpu.VMEM((slots, tokens), dtype)],
        compiler_params=pltpu.CompilerParams(vmem_limit_bytes=OWN_VMEM),
        cost_estimate=pl.CostEstimate(
            flops=2 * tokens * slots * width,
            bytes_accessed=2 * width * (tokens + slots),
            transcendentals=0,
        ),
        name="pack_rows",
    )(small, *rows)


def tile_rows(g):
    return pl.ds(SUBLANES * (g + 1), SUBLANES)


def forward_kernel(
    all_ref, *refs, groups, top_count, capacity, targets, cube
):
    (level_out, inverse_out, column_ref, seed_q_ref, seed_p_ref, where_ref,
     gate_ref, own_ref, dense_ref, before_ref, level_ref, inverse_ref, level_sem) = refs
    outgoing = [
        pltpu.make_async_copy(level_ref.at[k], level_out.at[k], level_sem.at[k])
        for k in range(ITERS + 1)
    ]
    outgoing.append(pltpu.make_async_copy(inverse_ref, inverse_out, level_sem.at[ITERS + 1]))
    devices = all_ref.shape[0]
    tiles = groups + 1
    me = lax.axis_index(AXES)

    def block(d):
        across = jnp.bitwise_xor(d, me)
        place = jnp.int32(0)
        for step, bit in enumerate(cube):
            flag = jnp.bitwise_and(lax.shift_right_logical(across, jnp.int32(bit)), 1)
            place = place + flag * (1 << step)
        return place

    tile = (SUBLANES, LANES)
    row_id = lax.broadcasted_iota(jnp.int32, tile, 0)
    zero = jnp.zeros(tile, jnp.float32)

    def totals(sums):
        out = []
        for i in range(tiles):
            column = jnp.sum(sums[i], 1, keepdims=True) + zero
            out.append(jnp.where(row_id < groups, column, 1.0) if i == 0 else column)
        return out

    def start(d, sums):
        new = []
        place = block(d)
        for i in range(tiles):
            rows = pl.ds(SUBLANES * i, SUBLANES)
            level = capped(all_ref[place, rows, :])
            if i == 0:
                level = jnp.where(row_id < groups, level, 0.0)
            level_ref[0, d, rows, :] = level
            new.append(sums[i] + level)
        named = [
            all_ref[place, groups + k : groups + k + 1, :].astype(jnp.int32)
            for k in range(top_count)
        ]
        for g in range(groups):
            expert = row_id + g * SUBLANES
            hit = named[0] == expert
            for k in range(1, top_count):
                hit = hit | (named[k] == expert)
            dense_ref[d, pl.ds(SUBLANES * g, SUBLANES), :] = hit.astype(jnp.float32)
        return tuple(new)

    sums = lax.fori_loop(0, devices, start, (zero,) * tiles, unroll=4)
    outgoing[0].start()

    for k in range(ITERS):
        columns = totals(sums)
        factors = []
        for i in range(tiles):
            column_ref[k, pl.ds(SUBLANES * i, SUBLANES), :] = columns[i]
            factors.append(targets[min(i, 1)] / columns[i])

        def step(d, sums, k=k, factors=factors):
            new = []
            for i in range(tiles):
                rows = pl.ds(SUBLANES * i, SUBLANES)
                scaled = level_ref[k, d, rows, :] * factors[i]
                inverse = 1.0 / jnp.sum(scaled, 0, keepdims=True)
                inverse_ref[k, d, pl.ds(i, 1), :] = inverse
                level = scaled * inverse
                level_ref[k + 1, d, rows, :] = level
                new.append(sums[i] + level)
            return tuple(new)

        sums = lax.fori_loop(0, devices, step, (zero,) * tiles, unroll=4)
        outgoing[k + 1].start()
    outgoing[ITERS + 1].start()

    experts = groups * SUBLANES
    earlier = (
        lax.broadcasted_iota(jnp.int32, (LANES, LANES), 0)
        < lax.broadcasted_iota(jnp.int32, (LANES, LANES), 1)
    ).astype(jnp.bfloat16)
    before_ref[...] = jnp.dot(
        dense_ref[...].reshape(devices * experts, LANES).astype(jnp.bfloat16),
        earlier,
        preferred_element_type=jnp.float32,
    ).reshape(devices, experts, LANES)

    per_block = LANES // capacity
    slot_id = lax.broadcasted_iota(jnp.int32, (capacity, LANES), 0)

    def finish(d, unused):
        picks = []
        total = jnp.zeros((1, LANES), jnp.float32)
        for g in range(groups):
            hit = dense_ref[d, pl.ds(SUBLANES * g, SUBLANES), :]
            pick_p = hit * level_ref[ITERS, d, g : g + 1, :]
            pick_q = hit * level_ref[ITERS, d, tile_rows(g), :]
            pair = pick_p * pick_q
            total = total + jnp.sum(pair, 0, keepdims=True)
            picks.append((pick_p, pick_q, pair))
        share = 1.0 / total
        hit_me = dense_ref[d, pl.ds(me, 1), :]
        before_me = before_ref[d, pl.ds(me, 1), :].astype(jnp.int32)
        for g in range(groups):
            rows = pl.ds(SUBLANES * g, SUBLANES)
            pick_p, pick_q, pair = picks[g]
            seed_q_ref[d, rows, :] = pick_p * share
            seed_p_ref[d, rows, :] = pick_q * share
            dense_ref[d, rows, :] = pair * share
            position = before_ref[d, rows, :].astype(jnp.int32)
            lane = lax.rem(d, per_block) * capacity + position
            where_ref[d, rows, :] = jnp.minimum(lane, LANES - 1)
        gate_me = dense_ref[d, pl.ds(me, 1), :].astype(jnp.bfloat16).astype(jnp.float32)
        taken = jnp.where((before_me == slot_id) & (hit_me > 0.0), gate_me, 0.0)
        gate_ref[pl.ds(d * capacity, capacity), :] = jnp.sum(taken, 1, keepdims=True) + jnp.zeros(
            (capacity, LANES), jnp.float32
        )
        return unused

    lax.fori_loop(0, devices, finish, 0, unroll=4)
    for i in range(tiles):
        rows = pl.ds(SUBLANES * i, SUBLANES)
        logits = all_ref[0, rows, :]
        own_ref[rows, :] = level_ref[0, me, rows, :] * squashing(logits)
    for copy in outgoing:
        copy.wait()


def forward(everyone, cube, groups, top_count, capacity, targets):
    devices, rows, lanes = everyone.shape
    experts = groups * SUBLANES
    f32 = jnp.float32
    shapes = [
        ((ITERS + 1, devices, rows, lanes), f32),
        ((ITERS, devices, SUBLANES, lanes), f32),
        ((ITERS, rows, lanes), f32),
        ((devices, experts, lanes), f32),
        ((devices, experts, lanes), f32),
        ((devices, experts, lanes), jnp.int32),
        ((devices * capacity, lanes), f32),
        ((rows, lanes), f32),
    ]
    vmem = pl.BlockSpec(memory_space=pltpu.VMEM)
    return pl.pallas_call(
        partial(
            forward_kernel,
            groups=groups,
            top_count=top_count,
            capacity=capacity,
            targets=targets,
            cube=cube,
        ),
        out_shape=[jax.ShapeDtypeStruct(s, d) for s, d in shapes],
        in_specs=[vmem],
        out_specs=[pl.BlockSpec(memory_space=pl.ANY)] * 2 + [vmem] * (len(shapes) - 2),
        scratch_shapes=[
            pltpu.VMEM((devices, experts, lanes), f32),
            pltpu.VMEM((devices, experts, lanes), f32),
            pltpu.VMEM(shapes[0][0], f32),
            pltpu.VMEM(shapes[1][0], f32),
            pltpu.SemaphoreType.DMA((ITERS + 2,)),
        ],
        cost_estimate=pl.CostEstimate(flops=10_000_000, bytes_accessed=8_000_000, transcendentals=0),
        name="forward",
    )(everyone)


def product_kernel(table_ref, rows_ref, weight_ref, *refs, carried, last):
    refs = list(refs)
    unscaled = lax.dot_general(
        rows_ref[...],
        weight_ref[...],
        (((1,), (1,)), ((), ())),
        preferred_element_type=jnp.float32,
    )
    if carried:
        unscaled = unscaled + refs.pop(0)[...]
    if not last:
        refs[-1][...] = unscaled
        return
    saved_ref, gate_ref = refs[:2]
    grad_ref, slot_ref, sum_ref = refs[-3:]
    grad_ref[...] = (gate_ref[:, :1] * unscaled).astype(grad_ref.dtype)
    partial_sums = unscaled * saved_ref[...].astype(jnp.float32)
    folded = partial_sums[:, :LANES]
    for j in range(1, partial_sums.shape[1] // LANES):
        folded = folded + partial_sums[:, j * LANES : (j + 1) * LANES]
    first = pl.program_id(0) == 0

    @pl.when(first)
    def _():
        sum_ref[...] = folded

    @pl.when(jnp.logical_not(first))
    def _():
        sum_ref[...] = sum_ref[...] + folded

    @pl.when(pl.program_id(0) == pl.num_programs(0) - 1)
    def _():
        sums = jnp.sum(sum_ref[...].T, 0, keepdims=True)
        for d in range(slot_ref.shape[0]):
            slot_ref[d, 0] = sums


def product(
    table, entry, rows, weight, saved, gates, copies, grant, earlier=(), part=0, carried=None,
    last=True
):
    slots, width = rows.shape
    hidden = weight.shape[0]
    total = saved.shape[0]
    block = 512 if hidden % 512 == 0 else hidden
    row_block = pl.BlockSpec((slots, block), lambda i, table: (table[entry], i))
    own_block = pl.BlockSpec((slots, block), lambda i, table: (0, i))
    operands = [rows, weight]
    in_specs = [
        pl.BlockSpec((slots, width), lambda i, table: (0, 0)),
        pl.BlockSpec((block, width), lambda i, table: (i, part)),
    ]
    if carried is not None:
        operands.append(carried)
        in_specs.append(own_block)
    if last:
        operands += [saved, gates]
        in_specs += [row_block, pl.BlockSpec((slots, LANES), lambda i, table: (table[entry], 0))]
        out_shape = [
            jax.ShapeDtypeStruct((total, hidden), jnp.bfloat16),
            jax.ShapeDtypeStruct((copies, total // slots, 1, slots), jnp.float32),
        ]
        out_specs = [
            row_block,
            pl.BlockSpec((copies, 1, 1, slots), lambda i, table: (0, table[entry], 0, 0)),
        ]
        scratch = [pltpu.VMEM((slots, LANES), jnp.float32)]
    else:
        out_shape = jax.ShapeDtypeStruct((slots, hidden), jnp.float32)
        out_specs = own_block
        scratch = []
    first = 1 + len(operands)
    return pl.pallas_call(
        partial(product_kernel, carried=carried is not None, last=last),
        out_shape=out_shape,
        grid_spec=pltpu.PrefetchScalarGridSpec(
            num_scalar_prefetch=1,
            grid=(hidden // block,),
            in_specs=in_specs + [pl.BlockSpec(memory_space=pl.ANY)] * len(earlier),
            out_specs=out_specs,
            scratch_shapes=scratch,
        ),
        input_output_aliases={first + i: i for i in range(len(earlier))},
        compiler_params=pltpu.CompilerParams(vmem_limit_bytes=grant),
        cost_estimate=pl.CostEstimate(
            flops=2 * slots * width * hidden,
            bytes_accessed=2 * (slots * width + hidden * width + 2 * slots * hidden),
            transcendentals=0,
        ),
        name="product",
    )(table, *operands, *earlier)


def adjoint_kernel(
    answer_ref, level_ref, inverse_ref, column_ref, seed_q_ref, seed_p_ref, where_ref,
    own_ref, group_ref, expert_ref, carry_ref, slot_ref, *, groups, capacity, targets
):
    devices = level_ref.shape[1]
    tiles = groups + 1
    tile = (SUBLANES, LANES)
    row_id = lax.broadcasted_iota(jnp.int32, tile, 0)
    zero = jnp.zeros(tile, jnp.float32)
    per_block = LANES // capacity
    width = answer_ref.shape[3]
    for e in range(answer_ref.shape[0]):
        for h in range(answer_ref.shape[1]):
            slot_ref[e : e + 1, h * width : (h + 1) * width] = answer_ref[e, h]

    def seeds(d):
        block = pl.ds(pl.multiple_of(lax.div(d, per_block) * LANES, LANES), LANES)
        grads = []
        mixed = jnp.zeros((1, LANES), jnp.float32)
        for g in range(groups):
            rows = pl.ds(SUBLANES * g, SUBLANES)
            grad = jnp.take_along_axis(slot_ref[rows, block], where_ref[d, rows, :], axis=1)
            gate = seed_q_ref[d, rows, :] * level_ref[ITERS, d, tile_rows(g), :]
            mixed = mixed + jnp.sum(gate * grad, 0, keepdims=True)
            grads.append(grad)
        out = [zero]
        for g in range(groups):
            rows = pl.ds(SUBLANES * g, SUBLANES)
            grad = grads[g] - mixed
            out.append(seed_q_ref[d, rows, :] * grad)
            level = jnp.sum(seed_p_ref[d, rows, :] * grad, 0, keepdims=True)
            out[0] = jnp.where(row_id == g, level, out[0])
        return out

    def factors_of(k):
        out = []
        for i in range(tiles):
            column = column_ref[k, pl.ds(SUBLANES * i, SUBLANES), :]
            factor = targets[min(i, 1)] / column
            if i == 0:
                factor = jnp.where(row_id < groups, factor, 0.0)
            out.append((factor, column))
        return out

    inner = None
    for k in reversed(range(ITERS)):
        if inner is not None:
            scale = []
            for i, (factor, column) in enumerate(factors_of(k + 1)):
                total = jnp.sum(inner[i], 1, keepdims=True) + zero
                scale.append((factor, total / column))

        def step(d, sums, k=k):
            if k == ITERS - 1:
                grads = seeds(d)
            else:
                grads = [
                    scale[i][0] * (carry_ref[d, pl.ds(SUBLANES * i, SUBLANES), :] - scale[i][1])
                    for i in range(tiles)
                ]
            new = []
            for i in range(tiles):
                rows = pl.ds(SUBLANES * i, SUBLANES)
                along = jnp.sum(grads[i] * level_ref[k + 1, d, rows, :], 0, keepdims=True)
                scaled = (grads[i] - along) * inverse_ref[k, d, pl.ds(i, 1), :]
                carry_ref[d, rows, :] = scaled
                new.append(sums[i] + scaled * level_ref[k, d, rows, :])
            return tuple(new)

        inner = lax.fori_loop(0, devices, step, (zero,) * tiles, unroll=4)

    me = lax.axis_index(AXES)
    for i, (factor, column) in enumerate(factors_of(0)):
        rows = pl.ds(SUBLANES * i, SUBLANES)
        total = jnp.sum(inner[i], 1, keepdims=True) + zero
        carry_ref[0, rows, :] = (
            factor * (carry_ref[me, rows, :] - total / column) * own_ref[rows, :]
        )
    group_ref[...] = carry_ref[0, :groups, :]
    expert_ref[...] = carry_ref[0, SUBLANES:, :]


def adjoint(slot_grads, saved, own, groups, capacity, targets):
    level = saved[0]
    _, lanes = level.shape[2:]
    vmem = pl.BlockSpec(memory_space=pltpu.VMEM)
    return pl.pallas_call(
        partial(adjoint_kernel, groups=groups, capacity=capacity, targets=targets),
        out_shape=[
            jax.ShapeDtypeStruct((groups, lanes), jnp.float32),
            jax.ShapeDtypeStruct((groups * SUBLANES, lanes), jnp.float32),
        ],
        in_specs=[vmem] * (2 + len(saved)),
        out_specs=[vmem, vmem],
        scratch_shapes=[
            pltpu.VMEM(level.shape[1:], jnp.float32),
            pltpu.VMEM((groups * SUBLANES, level.shape[1] * capacity), jnp.float32),
        ],
        compiler_params=pltpu.CompilerParams(vmem_limit_bytes=24 << 20),
        cost_estimate=pl.CostEstimate(flops=10_000_000, bytes_accessed=8_000_000, transcendentals=0),
        name="adjoint",
    )(slot_grads, *saved, own)


def column_parts(width):
    return 2 if width % (2 * LANES) == 0 else 1


def cube_bits(groups, per_group):
    low = per_group.bit_length() - 1
    high = (groups * per_group).bit_length() - 1
    return [*range(low, high), *range(low)]


def replicated(group_logits, expert_logits, expert_ids, cotangent, hidden_saved, w_down):
    groups = lax.axis_size(("half", "plane"))
    per_group = lax.axis_size("expert")
    near = lax.axis_size(NEAR)
    experts = groups * per_group
    tokens_here, top_count = expert_ids.shape
    width = cotangent.shape[1]
    capacity = hidden_saved.shape[1] // experts
    targets = (float(tokens_here * per_group), float(tokens_here * groups))
    half = lax.axis_index("half")
    table = jnp.stack([half, 1 - half]).astype(jnp.int32)

    planes = lax.axis_size("plane")

    parts = column_parts(width)

    mine, own_packed, *cut_rows = first_rows(
        group_logits, expert_ids, expert_logits, cotangent, near, capacity, parts
    )
    column = [mine]
    for across in range(1, groups):
        pairs = [(d, d ^ (across * per_group)) for d in range(experts)]
        column.append(lax.ppermute(mine, AXES, pairs))
    other = column[planes]
    cube = cube_bits(groups, per_group)
    everyone = jnp.stack(column)
    for bit in cube[groups.bit_length() - 1 :]:
        pairs = [(d, d ^ (1 << bit)) for d in range(experts)]
        everyone = jnp.concatenate([everyone, lax.ppermute(everyone, AXES, pairs)])

    swapped = []
    for i, block in enumerate(cut_rows):
        swapped.append([])
        for j in range(planes):
            up, down = (j, j + planes), (2 * planes - 1 - j, planes - 1 - j)
            swapped[i].append(lax.ppermute(block, ("half", "plane"), [up, down]))

    def send(packed):
        packed = packed.reshape(near, capacity, -1)
        got = lax.all_to_all(packed, NEAR, split_axis=0, concat_axis=0)
        return got.reshape(near * capacity, -1)

    weight, hidden = w_down[0], hidden_saved[0]
    own_rows = send(own_packed)
    other_rows = []
    for i in range(parts):
        other_packed = pack_rows(other, swapped[i], near, capacity, groups, top_count)
        other_rows.append(send(other_packed))
    *saved, gates, own = forward(everyone, cube, groups, top_count, capacity, targets)
    result = product(table, 0, own_rows, weight, hidden, gates, experts, OWN_VMEM)
    carried = None
    for i in range(parts):
        last = i == parts - 1
        carried = product(
            table, 1, other_rows[i], weight, hidden, gates, experts,
            OTHER_VMEM if last else OWN_VMEM, result if last else (), i, carried, last,
        )
    result = carried
    hidden_grad, slot_grad = result
    slot_grads = lax.all_to_all(slot_grad, AXES, split_axis=0, concat_axis=0)
    d_group, d_expert = adjoint(slot_grads, saved, own, groups, capacity, targets)
    return (hidden_grad[None], d_group.T, d_expert.T)


def per_device(group_logits, expert_logits, expert_ids, cotangent, hidden_saved, w_down):
    groups = lax.axis_size(("half", "plane"))
    per_group = lax.axis_size("expert")
    tokens_here, top_count = expert_ids.shape
    capacity = hidden_saved.shape[1] // (groups * per_group)
    everyone_bytes = 4 * tokens_here * (groups * per_group) * (groups * per_group + SUBLANES)
    fits = (
        tokens_here == LANES
        and groups in (2, 4)
        and column_parts(cotangent.shape[1]) == 2
        and per_group == SUBLANES
        and groups + top_count <= SUBLANES
        and LANES % capacity == 0
        and capacity % SUBLANES == 0
        and everyone_bytes <= REPLICATED_BYTES
    )
    form = replicated if fits else distributed
    return form(group_logits, expert_logits, expert_ids, cotangent, hidden_saved, w_down)


def solution(mesh):
    groups, per_group = mesh.shape["group"], mesh.shape["expert"]
    halves = 2 if groups % 2 == 0 else 1
    parts = Mesh(mesh.devices.reshape(halves, groups // halves, per_group), AXES)
    rows = P(AXES, None)
    blocks = P(AXES, None, None)
    return jax.shard_map(
        per_device,
        mesh=parts,
        in_specs=(rows, rows, rows, rows, blocks, blocks),
        out_specs=(blocks, rows, rows),
        check_vma=False,
    )
```

profile of v0, /device:TPU:0, one launch (start us, length us, event | category | flops | bytes accessed | tf_op | source)
XLA Modules:
  0.0 167.9 jit_solution(15559150549368665771)
XLA Ops:
  0.6 4.0 %first_rows.1 = (f32[40,128]{1,0:T(8,128)}, bf16[256,3584]{1,0:T(8,128)(2,1)}, bf16[128,1792]{1,0:T(8,128)(2,1)}, bf16[128,1792]{1,0:T(8,128)(2,1)}) custom-call(f32[4,128]{1,0:T(4,128)} %bitcast.49, s32[2,128]{1,0:T(2,128)} %bitcast.50, f32[32,128]{1,0:T(8,128)} %bitcast.48, bf16[128,3584]{1,0:T(8,128)(2,1)} %cotangent_ref.1), custom_call_target="tpu_custom_call" | custom-call | flops 234881024 | bytes 2752512 | tf_op jit(solution)/shard_map/first_rows/pallas_call | solution.py:230
  4.6 0.0 copy-start.16
  4.6 0.0 copy-start.15
  4.6 6.1 %collective-permute-start.3 = (bf16[128,1792]{1,0:T(8,128)(2,1)}, bf16[128,1792]{1,0:T(8,128)(2,1)S(1)}, u32[]{:S(2)}, u32[]{:S(2)}) collective-permute-start(bf16[128,1792]{1,0:T(8,128)(2,1)} %get-tuple-element.23), channel_id=1, source_target_pairs={{0,16},{24,8},{1,17},{25,9},{2,18},{26,10},{3,19},{27,11},{4,20},{... | collective-permute-start | bytes 1376264 | tf_op jit(solution)/shard_map/ppermute | solution.py:718
  10.7 1.3 collective-permute-start.4
  12.0 3.6 %collective-permute-start = (f32[40,128]{1,0:T(8,128)}, f32[40,128]{1,0:T(8,128)S(1)}, u32[]{:S(2)}, u32[]{:S(2)}) collective-permute-start(f32[40,128]{1,0:T(8,128)} %get-tuple-element.21), channel_id=1, source_target_pairs={{0,16},{1,17},{2,18},{3,19},{4,20},{5,21},{6,22},{7,23},{8,24},{9,... | collective-permute-start | bytes 61448 | tf_op jit(solution)/shard_map/ppermute | solution.py:705
  15.7 17.5 %collective-permute-done.small_ref = f32[40,128]{1,0:T(8,128)S(1)} collective-permute-done((f32[40,128]{1,0:T(8,128)}, f32[40,128]{1,0:T(8,128)S(1)}, u32[]{:S(2)}, u32[]{:S(2)}) %collective-permute-start) | collective-permute-done | bytes 20512 | tf_op jit(solution)/shard_map/ppermute | solution.py:705
  33.2 0.0 collective-permute-done.3.refs_0_
  33.2 0.0 collective-permute-done.4.refs_1_
  33.2 0.9 pack_rows.3
  34.1 18.5 %all_to_all.20 = bf16[16,16,1792]{2,1,0:T(8,128)(2,1)} all-to-all(bf16[16,16,1792]{2,1,0:T(8,128)(2,1)S(1)} %bitcast.41), channel_id=1, replica_groups=mesh['half'=2,'plane'=2,'expert'=8] {'plane','expert'}, dimensions={0} | all-to-all | bytes 1835008 | tf_op jit(solution)/shard_map/all_to_all | solution.py:722
  52.6 4.4 %all-to-all-start.2 = ((bf16[16,16,3584]{2,1,0:T(8,128)(2,1)}), bf16[16,16,3584]{2,1,0:T(8,128)(2,1)}, u32[]{:S(2)}, u32[]{:S(2)}) async-start(bf16[16,16,3584]{2,1,0:T(8,128)(2,1)} %bitcast.43), calls=%async_computation.2 | async-start | bytes 3670016 | tf_op jit(solution)/shard_map/all_to_all | solution.py:722
  57.0 0.0 copy-done.16
  57.0 4.4 %collective-permute-start.1 = (bf16[128,1792]{1,0:T(8,128)(2,1)S(1)}, bf16[128,1792]{1,0:T(8,128)(2,1)S(1)}, u32[]{:S(2)}, u32[]{:S(2)}) collective-permute-start(bf16[128,1792]{1,0:T(8,128)(2,1)S(1)} %copy-done.16), channel_id=1, source_target_pairs={{0,16},{24,8},{1,17},{25,9},{2,18},{26,10},{3,19},{27,11},{4,20},{... | collective-permute-start | bytes 1376264 | tf_op jit(solution)/shard_map/ppermute | solution.py:718
  61.5 1.3 collective-permute-start.2
  62.8 0.0 copy-done.15
  62.8 3.0 %collective-permute-start.5 = (f32[40,128]{1,0:T(8,128)S(1)}, f32[40,128]{1,0:T(8,128)S(1)}, u32[]{:S(2)}, u32[]{:S(2)}) collective-permute-start(f32[40,128]{1,0:T(8,128)S(1)} %copy-done.15), channel_id=1, source_target_pairs={{0,8},{1,9},{2,10},{3,11},{4,12},{5,13},{6,14},{7,15},{8,0},{9,1},... | collective-permute-start | bytes 61448 | tf_op jit(solution)/shard_map/ppermute | solution.py:705
  65.7 2.1 %collective-permute-start.6 = (f32[40,128]{1,0:T(8,128)S(1)}, f32[40,128]{1,0:T(8,128)S(1)}, u32[]{:S(2)}, u32[]{:S(2)}) collective-permute-start(f32[40,128]{1,0:T(8,128)S(1)} %copy-done.15), channel_id=1, source_target_pairs={{0,24},{1,25},{2,26},{3,27},{4,28},{5,29},{6,30},{7,31},{8,16},{9,... | collective-permute-start | bytes 61448 | tf_op jit(solution)/shard_map/ppermute | solution.py:705
  67.9 0.6 constant_dynamic-update-slice_fusion.10
  68.5 21.7 %collective-permute-done.5 = f32[40,128]{1,0:T(8,128)S(1)} collective-permute-done((f32[40,128]{1,0:T(8,128)S(1)}, f32[40,128]{1,0:T(8,128)S(1)}, u32[]{:S(2)}, u32[]{:S(2)}) %collective-permute-start.5) | collective-permute-done | bytes 20512 | tf_op jit(solution)/shard_map/ppermute | solution.py:705
  90.1 2.9 %collective-permute-done.6 = f32[40,128]{1,0:T(8,128)S(1)} collective-permute-done((f32[40,128]{1,0:T(8,128)S(1)}, f32[40,128]{1,0:T(8,128)S(1)}, u32[]{:S(2)}, u32[]{:S(2)}) %collective-permute-start.6) | collective-permute-done | bytes 20512 | tf_op jit(solution)/shard_map/ppermute | solution.py:705
  93.1 0.1 collective-permute-start.7
  93.1 0.0 collective-permute-done.1.refs_0_
  93.1 0.0 collective-permute-done.2.refs_1_
  93.2 0.0 slice-start
  93.2 0.9 pack_rows.2
  94.1 0.0 copy-start.5
  94.1 1.0 copy-done.5
  95.1 0.0 all-to-all-done.2
  95.1 5.0 %all-to-all-start = ((bf16[16,16,1792]{2,1,0:T(8,128)(2,1)}), bf16[16,16,1792]{2,1,0:T(8,128)(2,1)}, u32[]{:S(2)}, u32[]{:S(2)}) async-start(bf16[16,16,1792]{2,1,0:T(8,128)(2,1)} %bitcast.40), calls=%async_computation | async-start | bytes 1835008 | tf_op jit(solution)/shard_map/all_to_all | solution.py:722
  100.1 0.6 constant_dynamic-update-slice_fusion.9
  100.7 0.6 constant_dynamic-update-slice_fusion.8
  101.4 0.6 constant_dynamic-update-slice_fusion.7
  102.0 0.0 collective-permute-done.7
  102.0 0.7 constant_dynamic-update-slice_fusion.6
  102.7 2.7 %collective-permute-start.8 = (f32[8,40,128]{2,1,0:T(8,128)S(1)}, f32[8,40,128]{2,1,0:T(8,128)S(1)}, u32[]{:S(2)}, u32[]{:S(2)}) collective-permute-start(f32[8,40,128]{2,1,0:T(8,128)S(1)} %get-tuple-element.43), channel_id=1, source_target_pairs={{0,2},{1,3},{2,0},{3,1},{4,6},{5,7},{6,4},{7,5},{8,10},{9,11},{10,... | collective-permute-start | bytes 491528 | tf_op jit(solution)/shard_map/ppermute | solution.py:711
  105.4 12.2 %collective-permute-done.8 = f32[8,40,128]{2,1,0:T(8,128)S(1)} collective-permute-done((f32[8,40,128]{2,1,0:T(8,128)S(1)}, f32[8,40,128]{2,1,0:T(8,128)S(1)}, u32[]{:S(2)}, u32[]{:S(2)}) %collective-permute-start.8) | collective-permute-done | bytes 163872 | tf_op jit(solution)/shard_map/ppermute | solution.py:711
  117.6 0.7 constant_dynamic-update-slice_fusion.5
  118.3 0.4 collective-permute-start.9
  118.7 0.1 pad_add_fusion.table_ref
  118.8 9.4 %collective-permute-done.9 = f32[16,40,128]{2,1,0:T(8,128)S(1)} collective-permute-done((f32[16,40,128]{2,1,0:T(8,128)}, f32[16,40,128]{2,1,0:T(8,128)S(1)}, u32[]{:S(2)}, u32[]{:S(2)}) %collective-permute-start.9) | collective-permute-done | bytes 327712 | tf_op jit(solution)/shard_map/ppermute | solution.py:711
  128.2 0.7 constant_dynamic-update-slice_fusion.11.all_ref
  129.0 6.0 %forward.1 = (f32[6,32,40,128]{3,2,1,0:T(8,128)}, f32[5,32,8,128]{3,2,1,0:T(8,128)}, f32[5,40,128]{2,1,0:T(8,128)}, f32[32,32,128]{2,1,0:T(8,128)}, f32[32,32,12...) custom-call(f32[32,40,128]{2,1,0:T(8,128)} %constant_dynamic-update-slice_fusion.11.all_ref), custom_call_target="tpu_custom_call" | custom-call | flops 10000000 | bytes 8000000 | tf_op jit(solution)/shard_map/forward/pallas_call | solution.py:452
  135.0 0.0 copy-start
  135.0 3.1 %copy-done = bf16[1,1024,3584]{2,1,0:T(8,128)(2,1)S(1)} copy-done((bf16[1,1024,3584]{2,1,0:T(8,128)(2,1)S(1)}, bf16[1,1024,3584]{2,1,0:T(8,128)(2,1)}, u32[]{:S(2)}) %copy-start) | copy-done | bytes 7340056
  138.1 1.2 copy-done.4
  139.3 2.2 %product.3.refs_0_ = f32[256,1024]{1,0:T(8,128)S(1)} custom-call(s32[2]{0:T(128)S(1)} %pad_add_fusion.table_ref, bf16[256,1792]{1,0:T(8,128)(2,1)S(1)} %bitcast.39, bf16[1024,3584]{1,0:T(8,128)(2,1)S(1)} %bitcast.33), custom_call_target="tpu_custom_call" | custom-call | flops 939524096 | bytes 5636096 | tf_op jit(solution)/shard_map/product/pallas_call | solution.py:548
  141.5 0.0 copy-start.1
  141.6 1.0 copy-done.1
  142.5 0.0 copy-done.14
  142.6 0.0 slice-done
  142.6 0.0 slice-done.1
  142.6 0.0 copy-done.2
  142.6 0.0 copy-done.6
  142.6 5.3 %product.4 = (bf16[512,1024]{1,0:T(8,128)(2,1)}, f32[32,2,1,256]{3,2,1,0:T(1,128)S(1)}) custom-call(s32[2]{0:T(128)S(1)} %pad_add_fusion.table_ref, bf16[256,3584]{1,0:T(8,128)(2,1)} %bitcast.16.rows_ref, bf16[1024,3584]{1,0:T(8,128)(2,1)S(1)} %bitcast.36, bf16[512,1024]{1,0:T(8,128)(2,1)S(1)} %bitcast.38, f32[512,128]{1,0:T(8,128)S(1)} %copy-done.6), custom_call_target="tpu_custom_call" | custom-call | flops 1879048192 | bytes 10223616 | tf_op jit(solution)/shard_map/product/pallas_call | solution.py:548
  147.9 0.6 copy-done.11
  148.5 0.0 all-to-all-done
  148.5 0.0 copy-start.9
  148.5 0.0 copy-start.10
  148.5 0.0 copy-start.12
  148.5 5.7 %product.5 = (bf16[512,1024]{1,0:T(8,128)(2,1)}, f32[32,2,1,256]{3,2,1,0:T(1,128)}) custom-call(s32[2]{0:T(128)} %copy-done.14, bf16[256,1792]{1,0:T(8,128)(2,1)} %bitcast.6.rows_ref, bf16[1024,3584]{1,0:T(8,128)(2,1)} %bitcast.32, f32[256,1024]{1,0:T(8,128)} %copy-done.1, bf16[512,1024]{1,0:T(8,128)(2,1)} %bitcast.37, ...), custom_call_target="tpu_custom_call", output_to_operand_aliasing={{0}: (6, {}), {1}: (7, {})} | custom-call | flops 939524096 | bytes 5636096 | tf_op jit(solution)/shard_map/product/pallas_call | solution.py:548
  154.2 10.0 %all_to_all.21.answer_ref = f32[32,2,1,256]{3,2,1,0:T(1,128)S(1)} all-to-all(f32[32,2,1,256]{3,2,1,0:T(1,128)} %get-tuple-element.29), channel_id=1, replica_groups=mesh['half'=2,'plane'=2,'expert'=8] {'half','plane','expert'}, dimensions={0} | all-to-all | bytes 131072 | tf_op jit(solution)/shard_map/all_to_all | solution.py:742
  164.2 0.0 copy-done.7
  164.3 3.6 %adjoint.1 = (f32[4,128]{1,0:T(4,128)}, f32[32,128]{1,0:T(8,128)}) custom-call(f32[32,2,1,256]{3,2,1,0:T(1,128)S(1)} %all_to_all.21.answer_ref, f32[6,32,40,128]{3,2,1,0:T(8,128)S(1)} %copy-done.3, f32[5,32,8,128]{3,2,1,0:T(8,128)S(1)} %copy-done.7, f32[5,40,128]{2,1,0:T(8,128)S(1)} %copy-done.12, f32[32,32,128]{2,1,0:T(8,128)S(1)} %copy-done.8, ...), custom_call_target="tpu_custom_call" | custom-call | flops 10000000 | bytes 8000000 | tf_op jit(solution)/shard_map/adjoint/pallas_call | solution.py:655
  (18 shorter events, 0.0 us)
Async XLA Ops:
  4.6 52.4 %copy-start.16 = (bf16[128,1792]{1,0:T(8,128)(2,1)S(1)}, bf16[128,1792]{1,0:T(8,128)(2,1)}, u32[]{:S(2)}) copy-start(bf16[128,1792]{1,0:T(8,128)(2,1)} %get-tuple-element.22) | copy-start | bytes 1376260
  4.6 58.2 %copy-start.15 = (f32[40,128]{1,0:T(8,128)S(1)}, f32[40,128]{1,0:T(8,128)}, u32[]{:S(2)}) copy-start(f32[40,128]{1,0:T(8,128)} %get-tuple-element.21) | copy-start | bytes 61444
  4.6 28.6 %collective-permute-start.3 = (bf16[128,1792]{1,0:T(8,128)(2,1)}, bf16[128,1792]{1,0:T(8,128)(2,1)S(1)}, u32[]{:S(2)}, u32[]{:S(2)}) collective-permute-start(bf16[128,1792]{1,0:T(8,128)(2,1)} %get-tuple-element.23), channel_id=1, source_target_pairs={{0,16},{24,8},{1,17},{25,9},{2,18},{26,10},{3,19},{27,11},{4,20},{... | collective-permute-start | bytes 1376264 | tf_op jit(solution)/shard_map/ppermute | solution.py:718
  10.7 22.5 %collective-permute-start.4 = (bf16[128,1792]{1,0:T(8,128)(2,1)}, bf16[128,1792]{1,0:T(8,128)(2,1)S(1)}, u32[]{:S(2)}, u32[]{:S(2)}) collective-permute-start(bf16[128,1792]{1,0:T(8,128)(2,1)} %get-tuple-element.23), channel_id=1, source_target_pairs={{8,24},{16,0},{9,25},{17,1},{10,26},{18,2},{11,27},{19,3},{12,28},... | collective-permute-start | bytes 1376264 | tf_op jit(solution)/shard_map/ppermute | solution.py:718
  12.0 21.2 %collective-permute-start = (f32[40,128]{1,0:T(8,128)}, f32[40,128]{1,0:T(8,128)S(1)}, u32[]{:S(2)}, u32[]{:S(2)}) collective-permute-start(f32[40,128]{1,0:T(8,128)} %get-tuple-element.21), channel_id=1, source_target_pairs={{0,16},{1,17},{2,18},{3,19},{4,20},{5,21},{6,22},{7,23},{8,24},{9,... | collective-permute-start | bytes 61448 | tf_op jit(solution)/shard_map/ppermute | solution.py:705
  52.6 42.5 %all-to-all-start.2 = ((bf16[16,16,3584]{2,1,0:T(8,128)(2,1)}), bf16[16,16,3584]{2,1,0:T(8,128)(2,1)}, u32[]{:S(2)}, u32[]{:S(2)}) async-start(bf16[16,16,3584]{2,1,0:T(8,128)(2,1)} %bitcast.43), calls=%async_computation.2 | async-start | bytes 3670016 | tf_op jit(solution)/shard_map/all_to_all | solution.py:722
  57.0 36.1 %collective-permute-start.1 = (bf16[128,1792]{1,0:T(8,128)(2,1)S(1)}, bf16[128,1792]{1,0:T(8,128)(2,1)S(1)}, u32[]{:S(2)}, u32[]{:S(2)}) collective-permute-start(bf16[128,1792]{1,0:T(8,128)(2,1)S(1)} %copy-done.16), channel_id=1, source_target_pairs={{0,16},{24,8},{1,17},{25,9},{2,18},{26,10},{3,19},{27,11},{4,20},{... | collective-permute-start | bytes 1376264 | tf_op jit(solution)/shard_map/ppermute | solution.py:718
  61.5 31.7 %collective-permute-start.2 = (bf16[128,1792]{1,0:T(8,128)(2,1)S(1)}, bf16[128,1792]{1,0:T(8,128)(2,1)S(1)}, u32[]{:S(2)}, u32[]{:S(2)}) collective-permute-start(bf16[128,1792]{1,0:T(8,128)(2,1)S(1)} %copy-done.16), channel_id=1, source_target_pairs={{8,24},{16,0},{9,25},{17,1},{10,26},{18,2},{11,27},{19,3},{12,28},... | collective-permute-start | bytes 1376264 | tf_op jit(solution)/shard_map/ppermute | solution.py:718
  62.8 27.4 %collective-permute-start.5 = (f32[40,128]{1,0:T(8,128)S(1)}, f32[40,128]{1,0:T(8,128)S(1)}, u32[]{:S(2)}, u32[]{:S(2)}) collective-permute-start(f32[40,128]{1,0:T(8,128)S(1)} %copy-done.15), channel_id=1, source_target_pairs={{0,8},{1,9},{2,10},{3,11},{4,12},{5,13},{6,14},{7,15},{8,0},{9,1},... | collective-permute-start | bytes 61448 | tf_op jit(solution)/shard_map/ppermute | solution.py:705
  65.7 27.3 %collective-permute-start.6 = (f32[40,128]{1,0:T(8,128)S(1)}, f32[40,128]{1,0:T(8,128)S(1)}, u32[]{:S(2)}, u32[]{:S(2)}) collective-permute-start(f32[40,128]{1,0:T(8,128)S(1)} %copy-done.15), channel_id=1, source_target_pairs={{0,24},{1,25},{2,26},{3,27},{4,28},{5,29},{6,30},{7,31},{8,16},{9,... | collective-permute-start | bytes 61448 | tf_op jit(solution)/shard_map/ppermute | solution.py:705
  93.1 8.9 %collective-permute-start.7 = (f32[4,40,128]{2,1,0:T(8,128)S(1)}, f32[4,40,128]{2,1,0:T(8,128)S(1)}, u32[]{:S(2)}, u32[]{:S(2)}) collective-permute-start(f32[4,40,128]{2,1,0:T(8,128)S(1)} %pad_maximum_fusion), channel_id=1, source_target_pairs={{0,1},{1,0},{2,3},{3,2},{4,5},{5,4},{6,7},{7,6},{8,9},{9,8},{10,11... | collective-permute-start | bytes 245768 | tf_op jit(solution)/shard_map/ppermute | solution.py:711
  93.2 49.4 %slice-start = ((s8[7340032]{0:T(1024)(128)(4,1)}), s8[3145728]{0:T(1024)(128)(4,1)S(1)}, s32[]{:S(2)}) async-start(s8[7340032]{0:T(1024)(128)(4,1)} %bitcast.34), calls=%async_computation.4 | async-start | bytes 6291456
  94.1 1.0 copy-start.5
  95.1 53.4 %all-to-all-start = ((bf16[16,16,1792]{2,1,0:T(8,128)(2,1)}), bf16[16,16,1792]{2,1,0:T(8,128)(2,1)}, u32[]{:S(2)}, u32[]{:S(2)}) async-start(bf16[16,16,1792]{2,1,0:T(8,128)(2,1)} %bitcast.40), calls=%async_computation | async-start | bytes 1835008 | tf_op jit(solution)/shard_map/all_to_all | solution.py:722
  102.7 14.9 %collective-permute-start.8 = (f32[8,40,128]{2,1,0:T(8,128)S(1)}, f32[8,40,128]{2,1,0:T(8,128)S(1)}, u32[]{:S(2)}, u32[]{:S(2)}) collective-permute-start(f32[8,40,128]{2,1,0:T(8,128)S(1)} %get-tuple-element.43), channel_id=1, source_target_pairs={{0,2},{1,3},{2,0},{3,1},{4,6},{5,7},{6,4},{7,5},{8,10},{9,11},{10,... | collective-permute-start | bytes 491528 | tf_op jit(solution)/shard_map/ppermute | solution.py:711
  118.3 9.9 %collective-permute-start.9 = (f32[16,40,128]{2,1,0:T(8,128)}, f32[16,40,128]{2,1,0:T(8,128)S(1)}, u32[]{:S(2)}, u32[]{:S(2)}) collective-permute-start(f32[16,40,128]{2,1,0:T(8,128)} %get-tuple-element.39), channel_id=1, source_target_pairs={{0,4},{1,5},{2,6},{3,7},{4,0},{5,1},{6,2},{7,3},{8,12},{9,13},{10,... | collective-permute-start | bytes 983048 | tf_op jit(solution)/shard_map/ppermute | solution.py:711
  118.8 23.8 %copy-start.14 = (s32[2]{0:T(128)}, s32[2]{0:T(128)S(1)}, u32[]{:S(2)}) copy-start(s32[2]{0:T(128)S(1)} %pad_add_fusion.table_ref) | copy-start | bytes 28
  135.0 3.1 %copy-start = (bf16[1,1024,3584]{2,1,0:T(8,128)(2,1)S(1)}, bf16[1,1024,3584]{2,1,0:T(8,128)(2,1)}, u32[]{:S(2)}) copy-start(bf16[1,1024,3584]{2,1,0:T(8,128)(2,1)} %param.11) | copy-start | bytes 22020100
  138.1 1.2 copy-start.4
  139.3 3.3 %slice-start.1 = ((s8[7340032]{0:T(1024)(128)(4,1)}), s8[4194304]{0:T(1024)(128)(4,1)S(1)}, s32[]{:S(2)}) async-start(s8[7340032]{0:T(1024)(128)(4,1)} %bitcast.34), calls=%async_computation.5 | async-start | bytes 8388608
  139.3 3.3 %copy-start.2 = (bf16[1,512,1024]{2,1,0:T(8,128)(2,1)S(1)}, bf16[1,512,1024]{2,1,0:T(8,128)(2,1)}, u32[]{:S(2)}) copy-start(bf16[1,512,1024]{2,1,0:T(8,128)(2,1)} %param.10) | copy-start | bytes 3145732
  139.3 3.3 %copy-start.6 = (f32[512,128]{1,0:T(8,128)S(1)}, f32[512,128]{1,0:T(8,128)}, u32[]{:S(2)}) copy-start(f32[512,128]{1,0:T(8,128)} %get-tuple-element.24.refs_1_.refs_2_) | copy-start | bytes 786436
  141.5 1.0 copy-start.1
  147.9 0.6 copy-start.11
  148.5 15.7 %copy-start.3 = (f32[6,32,40,128]{3,2,1,0:T(8,128)S(1)}, f32[6,32,40,128]{3,2,1,0:T(8,128)}, u32[]{:S(2)}) copy-start(f32[6,32,40,128]{3,2,1,0:T(8,128)} %get-tuple-element.30.level_ref) | copy-start | bytes 11796484
  148.5 15.7 %copy-start.7 = (f32[5,32,8,128]{3,2,1,0:T(8,128)S(1)}, f32[5,32,8,128]{3,2,1,0:T(8,128)}, u32[]{:S(2)}) copy-start(f32[5,32,8,128]{3,2,1,0:T(8,128)} %get-tuple-element.31.inverse_ref) | copy-start | bytes 1966084
  148.5 15.7 %copy-start.8 = (f32[32,32,128]{2,1,0:T(8,128)S(1)}, f32[32,32,128]{2,1,0:T(8,128)}, u32[]{:S(2)}) copy-start(f32[32,32,128]{2,1,0:T(8,128)} %get-tuple-element.33.seed_q_ref) | copy-start | bytes 1572868
  148.5 15.7 %copy-start.9 = (f32[32,32,128]{2,1,0:T(8,128)S(1)}, f32[32,32,128]{2,1,0:T(8,128)}, u32[]{:S(2)}) copy-start(f32[32,32,128]{2,1,0:T(8,128)} %get-tuple-element.34.seed_p_ref) | copy-start | bytes 1572868
  148.5 15.7 %copy-start.10 = (s32[32,32,128]{2,1,0:T(8,128)S(1)}, s32[32,32,128]{2,1,0:T(8,128)}, u32[]{:S(2)}) copy-start(s32[32,32,128]{2,1,0:T(8,128)} %get-tuple-element.35.where_ref) | copy-start | bytes 1572868
  148.5 15.7 %copy-start.12 = (f32[5,40,128]{2,1,0:T(8,128)S(1)}, f32[5,40,128]{2,1,0:T(8,128)}, u32[]{:S(2)}) copy-start(f32[5,40,128]{2,1,0:T(8,128)} %get-tuple-element.32.column_ref) | copy-start | bytes 307204
  148.5 15.7 %copy-start.13 = (f32[40,128]{1,0:T(8,128)S(1)}, f32[40,128]{1,0:T(8,128)}, u32[]{:S(2)}) copy-start(f32[40,128]{1,0:T(8,128)} %get-tuple-element.36.own_ref) | copy-start | bytes 61444
where the time goes:
time: 168 us
  waiting for transfers between devices  63.7 us (38%)
  starting transfers between devices  34.5 us (21%)
  Pallas kernels  28.7 us (17%)
  blocking collectives  28.4 us (17%)
  local copies, waits for them, and re-layouts  11.6 us (7%)
    ppermute x3, waiting for transfers between devices, replicated(): column.append(lax.ppermute(mine, AXES, pairs))  42.1 us
    ppermute x3, waiting for transfers between devices, replicated(): everyone = jnp.concatenate([everyone, lax.ppermute(everyone, AXES, pairs)])  21.6 us
    all_to_all x1, blocking collectives, send(): got = lax.all_to_all(packed, NEAR, split_axis=0, concat_axis=0)  18.5 us
    pallas_call x3, Pallas kernels, product(): pl.pallas_call(partial(product_kernel, carried=carried is not None, last=...  13.2 us
    ppermute x4, starting transfers between devices, replicated(): swapped[i].append(lax.ppermute(block, ('half', 'plane'), [up, down]))  13.1 us
    unnamed x43, local copies, waits for them, and re-layouts  10.1 us
    all_to_all x1, blocking collectives, replicated(): slot_grads = lax.all_to_all(slot_grad, AXES, split_axis=0, concat_axis=0)  9.98 us
    all_to_all x2, starting transfers between devices, send(): got = lax.all_to_all(packed, NEAR, split_axis=0, concat_axis=0)  9.43 us
  transfers between devices with their start and end apart: 12, of which 5 were waited for; matrix products, arithmetic and copies ran while one was open for 3% of the time, Pallas kernels for 9%

commit v1 on v0

--- a/solution.py
+++ b/solution.py
@@ -304,13 +304,12 @@
 def forward_kernel(
     all_ref, *refs, groups, top_count, capacity, targets, cube
 ):
-    (level_out, inverse_out, column_ref, seed_q_ref, seed_p_ref, where_ref,
-     gate_ref, own_ref, dense_ref, before_ref, level_ref, inverse_ref, level_sem) = refs
+    (level_out, inverse_ref, column_ref, seed_q_ref, seed_p_ref, where_ref,
+     gate_ref, own_ref, dense_ref, before_ref, level_ref, level_sem) = refs
     outgoing = [
         pltpu.make_async_copy(level_ref.at[k], level_out.at[k], level_sem.at[k])
         for k in range(ITERS + 1)
     ]
-    outgoing.append(pltpu.make_async_copy(inverse_ref, inverse_out, level_sem.at[ITERS + 1]))
     devices = all_ref.shape[0]
     tiles = groups + 1
     me = lax.axis_index(AXES)
@@ -380,7 +379,6 @@
 
         sums = lax.fori_loop(0, devices, step, (zero,) * tiles, unroll=4)
         outgoing[k + 1].start()
-    outgoing[ITERS + 1].start()
 
     experts = groups * SUBLANES
     earlier = (
@@ -406,15 +404,14 @@
             pair = pick_p * pick_q
             total = total + jnp.sum(pair, 0, keepdims=True)
             picks.append((pick_p, pick_q, pair))
-        share = 1.0 / total
         hit_me = dense_ref[d, pl.ds(me, 1), :]
         before_me = before_ref[d, pl.ds(me, 1), :].astype(jnp.int32)
         for g in range(groups):
             rows = pl.ds(SUBLANES * g, SUBLANES)
             pick_p, pick_q, pair = picks[g]
-            seed_q_ref[d, rows, :] = pick_p * share
-            seed_p_ref[d, rows, :] = pick_q * share
-            dense_ref[d, rows, :] = pair * share
+            seed_q_ref[d, rows, :] = pick_p / total
+            seed_p_ref[d, rows, :] = pick_q / total
+            dense_ref[d, rows, :] = pair / total
             position = before_ref[d, rows, :].astype(jnp.int32)
             lane = lax.rem(d, per_block) * capacity + position
             where_ref[d, rows, :] = jnp.minimum(lane, LANES - 1)
@@ -425,7 +422,7 @@
         )
         return unused
 
-    lax.fori_loop(0, devices, finish, 0, unroll=4)
+    lax.fori_loop(0, devices, finish, 0, unroll=2)
     for i in range(tiles):
         rows = pl.ds(SUBLANES * i, SUBLANES)
         logits = all_ref[0, rows, :]
@@ -460,13 +457,12 @@
         ),
         out_shape=[jax.ShapeDtypeStruct(s, d) for s, d in shapes],
         in_specs=[vmem],
-        out_specs=[pl.BlockSpec(memory_space=pl.ANY)] * 2 + [vmem] * (len(shapes) - 2),
+        out_specs=[pl.BlockSpec(memory_space=pl.ANY)] + [vmem] * (len(shapes) - 1),
         scratch_shapes=[
             pltpu.VMEM((devices, experts, lanes), f32),
             pltpu.VMEM((devices, experts, lanes), f32),
             pltpu.VMEM(shapes[0][0], f32),
-            pltpu.VMEM(shapes[1][0], f32),
-            pltpu.SemaphoreType.DMA((ITERS + 2,)),
+            pltpu.SemaphoreType.DMA((ITERS + 1,)),
         ],
         cost_estimate=pl.CostEstimate(flops=10_000_000, bytes_accessed=8_000_000, transcendentals=0),
         name="forward",
@@ -635,7 +631,7 @@
                 new.append(sums[i] + scaled * level_ref[k, d, rows, :])
             return tuple(new)
 
-        inner = lax.fori_loop(0, devices, step, (zero,) * tiles, unroll=4)
+        inner = lax.fori_loop(0, devices, step, (zero,) * tiles, unroll=8)
 
     me = lax.axis_index(AXES)
     for i, (factor, column) in enumerate(factors_of(0)):

time: 168 us -> 169 us (level)
  no operation moved by 1% of the time
where the time goes in v1:
time: 169 us; the launch traced here: 168 us
  waiting for transfers between devices  63.7 us (38%)
  starting transfers between devices  34.5 us (20%)
  Pallas kernels  29.1 us (17%)
  blocking collectives  28.4 us (17%)
  local copies, waits for them, and re-layouts  11.6 us (7%)
    ppermute x3, waiting for transfers between devices, replicated(): column.append(lax.ppermute(mine, AXES, pairs))  42.1 us
    ppermute x3, waiting for transfers between devices, replicated(): everyone = jnp.concatenate([everyone, lax.ppermute(everyone, AXES, pairs)])  21.6 us
    all_to_all x1, blocking collectives, send(): got = lax.all_to_all(packed, NEAR, split_axis=0, concat_axis=0)  18.5 us
    pallas_call x3, Pallas kernels, product(): pl.pallas_call(partial(product_kernel, carried=carried is not None, last=...  13.2 us
    ppermute x4, starting transfers between devices, replicated(): swapped[i].append(lax.ppermute(block, ('half', 'plane'), [up, down]))  13.1 us
    unnamed x43, local copies, waits for them, and re-layouts  10.1 us
    all_to_all x1, blocking collectives, replicated(): slot_grads = lax.all_to_all(slot_grad, AXES, split_axis=0, concat_axis=0)  9.98 us
    all_to_all x2, starting transfers between devices, send(): got = lax.all_to_all(packed, NEAR, split_axis=0, concat_axis=0)  9.43 us
  transfers between devices with their start and end apart: 12, of which 5 were waited for; matrix products, arithmetic and copies ran while one was open for 3% of the time, Pallas kernels for 9%

profile of v1, /device:TPU:0, one launch (start us, length us, event | category | flops | bytes accessed | tf_op | source)
XLA Modules:
  0.0 168.3 jit_solution(7561981347927350724)
XLA Ops:
  0.6 4.0 %first_rows.1 = (f32[40,128]{1,0:T(8,128)}, bf16[256,3584]{1,0:T(8,128)(2,1)}, bf16[128,1792]{1,0:T(8,128)(2,1)}, bf16[128,1792]{1,0:T(8,128)(2,1)}) custom-call(f32[4,128]{1,0:T(4,128)} %bitcast.49, s32[2,128]{1,0:T(2,128)} %bitcast.50, f32[32,128]{1,0:T(8,128)} %bitcast.48, bf16[128,3584]{1,0:T(8,128)(2,1)} %cotangent_ref.1), custom_call_target="tpu_custom_call" | custom-call | flops 234881024 | bytes 2752512 | tf_op jit(solution)/shard_map/first_rows/pallas_call | solution.py:230
  4.6 0.0 copy-start.16
  4.6 0.0 copy-start.15
  4.6 6.1 %collective-permute-start.3 = (bf16[128,1792]{1,0:T(8,128)(2,1)}, bf16[128,1792]{1,0:T(8,128)(2,1)S(1)}, u32[]{:S(2)}, u32[]{:S(2)}) collective-permute-start(bf16[128,1792]{1,0:T(8,128)(2,1)} %get-tuple-element.23), channel_id=1, source_target_pairs={{0,16},{24,8},{1,17},{25,9},{2,18},{26,10},{3,19},{27,11},{4,20},{... | collective-permute-start | bytes 1376264 | tf_op jit(solution)/shard_map/ppermute | solution.py:714
  10.7 1.3 collective-permute-start.4
  12.0 3.6 %collective-permute-start = (f32[40,128]{1,0:T(8,128)}, f32[40,128]{1,0:T(8,128)S(1)}, u32[]{:S(2)}, u32[]{:S(2)}) collective-permute-start(f32[40,128]{1,0:T(8,128)} %get-tuple-element.21), channel_id=1, source_target_pairs={{0,16},{1,17},{2,18},{3,19},{4,20},{5,21},{6,22},{7,23},{8,24},{9,... | collective-permute-start | bytes 61448 | tf_op jit(solution)/shard_map/ppermute | solution.py:701
  15.7 17.5 %collective-permute-done.small_ref = f32[40,128]{1,0:T(8,128)S(1)} collective-permute-done((f32[40,128]{1,0:T(8,128)}, f32[40,128]{1,0:T(8,128)S(1)}, u32[]{:S(2)}, u32[]{:S(2)}) %collective-permute-start) | collective-permute-done | bytes 20512 | tf_op jit(solution)/shard_map/ppermute | solution.py:701
  33.2 0.0 collective-permute-done.3.refs_0_
  33.2 0.0 collective-permute-done.4.refs_1_
  33.2 0.9 pack_rows.3
  34.1 18.5 %all_to_all.20 = bf16[16,16,1792]{2,1,0:T(8,128)(2,1)} all-to-all(bf16[16,16,1792]{2,1,0:T(8,128)(2,1)S(1)} %bitcast.41), channel_id=1, replica_groups=mesh['half'=2,'plane'=2,'expert'=8] {'plane','expert'}, dimensions={0} | all-to-all | bytes 1835008 | tf_op jit(solution)/shard_map/all_to_all | solution.py:718
  52.6 4.4 %all-to-all-start.2 = ((bf16[16,16,3584]{2,1,0:T(8,128)(2,1)}), bf16[16,16,3584]{2,1,0:T(8,128)(2,1)}, u32[]{:S(2)}, u32[]{:S(2)}) async-start(bf16[16,16,3584]{2,1,0:T(8,128)(2,1)} %bitcast.43), calls=%async_computation.2 | async-start | bytes 3670016 | tf_op jit(solution)/shard_map/all_to_all | solution.py:718
  57.0 0.0 copy-done.16
  57.0 4.4 %collective-permute-start.1 = (bf16[128,1792]{1,0:T(8,128)(2,1)S(1)}, bf16[128,1792]{1,0:T(8,128)(2,1)S(1)}, u32[]{:S(2)}, u32[]{:S(2)}) collective-permute-start(bf16[128,1792]{1,0:T(8,128)(2,1)S(1)} %copy-done.16), channel_id=1, source_target_pairs={{0,16},{24,8},{1,17},{25,9},{2,18},{26,10},{3,19},{27,11},{4,20},{... | collective-permute-start | bytes 1376264 | tf_op jit(solution)/shard_map/ppermute | solution.py:714
  61.5 1.3 collective-permute-start.2
  62.8 0.0 copy-done.15
  62.8 3.0 %collective-permute-start.5 = (f32[40,128]{1,0:T(8,128)S(1)}, f32[40,128]{1,0:T(8,128)S(1)}, u32[]{:S(2)}, u32[]{:S(2)}) collective-permute-start(f32[40,128]{1,0:T(8,128)S(1)} %copy-done.15), channel_id=1, source_target_pairs={{0,8},{1,9},{2,10},{3,11},{4,12},{5,13},{6,14},{7,15},{8,0},{9,1},... | collective-permute-start | bytes 61448 | tf_op jit(solution)/shard_map/ppermute | solution.py:701
  65.7 2.1 %collective-permute-start.6 = (f32[40,128]{1,0:T(8,128)S(1)}, f32[40,128]{1,0:T(8,128)S(1)}, u32[]{:S(2)}, u32[]{:S(2)}) collective-permute-start(f32[40,128]{1,0:T(8,128)S(1)} %copy-done.15), channel_id=1, source_target_pairs={{0,24},{1,25},{2,26},{3,27},{4,28},{5,29},{6,30},{7,31},{8,16},{9,... | collective-permute-start | bytes 61448 | tf_op jit(solution)/shard_map/ppermute | solution.py:701
  67.9 0.6 constant_dynamic-update-slice_fusion.10
  68.5 21.7 %collective-permute-done.5 = f32[40,128]{1,0:T(8,128)S(1)} collective-permute-done((f32[40,128]{1,0:T(8,128)S(1)}, f32[40,128]{1,0:T(8,128)S(1)}, u32[]{:S(2)}, u32[]{:S(2)}) %collective-permute-start.5) | collective-permute-done | bytes 20512 | tf_op jit(solution)/shard_map/ppermute | solution.py:701
  90.1 2.9 %collective-permute-done.6 = f32[40,128]{1,0:T(8,128)S(1)} collective-permute-done((f32[40,128]{1,0:T(8,128)S(1)}, f32[40,128]{1,0:T(8,128)S(1)}, u32[]{:S(2)}, u32[]{:S(2)}) %collective-permute-start.6) | collective-permute-done | bytes 20512 | tf_op jit(solution)/shard_map/ppermute | solution.py:701
  93.1 0.1 collective-permute-start.7
  93.1 0.0 collective-permute-done.1.refs_0_
  93.1 0.0 collective-permute-done.2.refs_1_
  93.2 0.0 slice-start
  93.2 0.9 pack_rows.2
  94.1 0.0 copy-start.5
  94.1 1.0 copy-done.5
  95.1 0.0 all-to-all-done.2
  95.1 5.0 %all-to-all-start = ((bf16[16,16,1792]{2,1,0:T(8,128)(2,1)}), bf16[16,16,1792]{2,1,0:T(8,128)(2,1)}, u32[]{:S(2)}, u32[]{:S(2)}) async-start(bf16[16,16,1792]{2,1,0:T(8,128)(2,1)} %bitcast.40), calls=%async_computation | async-start | bytes 1835008 | tf_op jit(solution)/shard_map/all_to_all | solution.py:718
  100.1 0.6 constant_dynamic-update-slice_fusion.9
  100.7 0.6 constant_dynamic-update-slice_fusion.8
  101.4 0.6 constant_dynamic-update-slice_fusion.7
  102.0 0.0 collective-permute-done.7
  102.0 0.7 constant_dynamic-update-slice_fusion.6
  102.7 2.7 %collective-permute-start.8 = (f32[8,40,128]{2,1,0:T(8,128)S(1)}, f32[8,40,128]{2,1,0:T(8,128)S(1)}, u32[]{:S(2)}, u32[]{:S(2)}) collective-permute-start(f32[8,40,128]{2,1,0:T(8,128)S(1)} %get-tuple-element.43), channel_id=1, source_target_pairs={{0,2},{1,3},{2,0},{3,1},{4,6},{5,7},{6,4},{7,5},{8,10},{9,11},{10,... | collective-permute-start | bytes 491528 | tf_op jit(solution)/shard_map/ppermute | solution.py:707
  105.4 12.2 %collective-permute-done.8 = f32[8,40,128]{2,1,0:T(8,128)S(1)} collective-permute-done((f32[8,40,128]{2,1,0:T(8,128)S(1)}, f32[8,40,128]{2,1,0:T(8,128)S(1)}, u32[]{:S(2)}, u32[]{:S(2)}) %collective-permute-start.8) | collective-permute-done | bytes 163872 | tf_op jit(solution)/shard_map/ppermute | solution.py:707
  117.6 0.7 constant_dynamic-update-slice_fusion.5
  118.3 0.4 collective-permute-start.9
  118.7 0.1 pad_add_fusion.table_ref
  118.8 9.4 %collective-permute-done.9 = f32[16,40,128]{2,1,0:T(8,128)S(1)} collective-permute-done((f32[16,40,128]{2,1,0:T(8,128)}, f32[16,40,128]{2,1,0:T(8,128)S(1)}, u32[]{:S(2)}, u32[]{:S(2)}) %collective-permute-start.9) | collective-permute-done | bytes 327712 | tf_op jit(solution)/shard_map/ppermute | solution.py:707
  128.2 0.7 constant_dynamic-update-slice_fusion.11.all_ref
  129.0 7.0 %forward.1 = (f32[6,32,40,128]{3,2,1,0:T(8,128)}, f32[5,32,8,128]{3,2,1,0:T(8,128)}, f32[5,40,128]{2,1,0:T(8,128)}, f32[32,32,128]{2,1,0:T(8,128)}, f32[32,32,12...) custom-call(f32[32,40,128]{2,1,0:T(8,128)} %constant_dynamic-update-slice_fusion.11.all_ref), custom_call_target="tpu_custom_call" | custom-call | flops 10000000 | bytes 8000000 | tf_op jit(solution)/shard_map/forward/pallas_call | solution.py:449
  135.9 0.0 copy-start
  136.0 3.1 %copy-done = bf16[1,1024,3584]{2,1,0:T(8,128)(2,1)S(1)} copy-done((bf16[1,1024,3584]{2,1,0:T(8,128)(2,1)S(1)}, bf16[1,1024,3584]{2,1,0:T(8,128)(2,1)}, u32[]{:S(2)}) %copy-start) | copy-done | bytes 7340056
  139.0 1.2 copy-done.4
  140.2 2.2 %product.3.refs_0_ = f32[256,1024]{1,0:T(8,128)S(1)} custom-call(s32[2]{0:T(128)S(1)} %pad_add_fusion.table_ref, bf16[256,1792]{1,0:T(8,128)(2,1)S(1)} %bitcast.39, bf16[1024,3584]{1,0:T(8,128)(2,1)S(1)} %bitcast.33), custom_call_target="tpu_custom_call" | custom-call | flops 939524096 | bytes 5636096 | tf_op jit(solution)/shard_map/product/pallas_call | solution.py:544
  142.5 0.0 copy-start.1
  142.5 1.0 copy-done.1
  143.5 0.0 copy-done.14
  143.5 0.0 slice-done
  143.5 0.0 slice-done.1
  143.5 0.0 copy-done.2
  143.5 5.3 %product.4 = (bf16[512,1024]{1,0:T(8,128)(2,1)}, f32[32,2,1,256]{3,2,1,0:T(1,128)S(1)}) custom-call(s32[2]{0:T(128)S(1)} %pad_add_fusion.table_ref, bf16[256,3584]{1,0:T(8,128)(2,1)} %bitcast.16.rows_ref, bf16[1024,3584]{1,0:T(8,128)(2,1)S(1)} %bitcast.36, bf16[512,1024]{1,0:T(8,128)(2,1)S(1)} %bitcast.38, f32[512,128]{1,0:T(8,128)S(1)} %copy-done.6), custom_call_target="tpu_custom_call" | custom-call | flops 1879048192 | bytes 10223616 | tf_op jit(solution)/shard_map/product/pallas_call | solution.py:544
  148.8 0.6 copy-done.11
  149.4 0.0 all-to-all-done
  149.4 5.7 %product.5 = (bf16[512,1024]{1,0:T(8,128)(2,1)}, f32[32,2,1,256]{3,2,1,0:T(1,128)}) custom-call(s32[2]{0:T(128)} %copy-done.14, bf16[256,1792]{1,0:T(8,128)(2,1)} %bitcast.6.rows_ref, bf16[1024,3584]{1,0:T(8,128)(2,1)} %bitcast.32, f32[256,1024]{1,0:T(8,128)} %copy-done.1, bf16[512,1024]{1,0:T(8,128)(2,1)} %bitcast.37, ...), custom_call_target="tpu_custom_call", output_to_operand_aliasing={{0}: (6, {}), {1}: (7, {})} | custom-call | flops 939524096 | bytes 5636096 | tf_op jit(solution)/shard_map/product/pallas_call | solution.py:544
  155.2 10.0 %all_to_all.21.answer_ref = f32[32,2,1,256]{3,2,1,0:T(1,128)S(1)} all-to-all(f32[32,2,1,256]{3,2,1,0:T(1,128)} %get-tuple-element.29), channel_id=1, replica_groups=mesh['half'=2,'plane'=2,'expert'=8] {'half','plane','expert'}, dimensions={0} | all-to-all | bytes 131072 | tf_op jit(solution)/shard_map/all_to_all | solution.py:738
  165.1 0.0 copy-done.8
  165.1 0.0 copy-done.9
  165.2 0.0 copy-done.10
  165.2 0.0 copy-done.12
  165.2 0.0 copy-done.13
  165.2 3.2 %adjoint.1 = (f32[4,128]{1,0:T(4,128)}, f32[32,128]{1,0:T(8,128)}) custom-call(f32[32,2,1,256]{3,2,1,0:T(1,128)S(1)} %all_to_all.21.answer_ref, f32[6,32,40,128]{3,2,1,0:T(8,128)S(1)} %copy-done.3, f32[5,32,8,128]{3,2,1,0:T(8,128)S(1)} %copy-done.7, f32[5,40,128]{2,1,0:T(8,128)S(1)} %copy-done.12, f32[32,32,128]{2,1,0:T(8,128)S(1)} %copy-done.8, ...), custom_call_target="tpu_custom_call" | custom-call | flops 10000000 | bytes 8000000 | tf_op jit(solution)/shard_map/adjoint/pallas_call | solution.py:651
  (18 shorter events, 0.0 us)
Async XLA Ops:
  4.6 52.4 %copy-start.16 = (bf16[128,1792]{1,0:T(8,128)(2,1)S(1)}, bf16[128,1792]{1,0:T(8,128)(2,1)}, u32[]{:S(2)}) copy-start(bf16[128,1792]{1,0:T(8,128)(2,1)} %get-tuple-element.22) | copy-start | bytes 1376260
  4.6 58.2 %copy-start.15 = (f32[40,128]{1,0:T(8,128)S(1)}, f32[40,128]{1,0:T(8,128)}, u32[]{:S(2)}) copy-start(f32[40,128]{1,0:T(8,128)} %get-tuple-element.21) | copy-start | bytes 61444
  4.6 28.6 %collective-permute-start.3 = (bf16[128,1792]{1,0:T(8,128)(2,1)}, bf16[128,1792]{1,0:T(8,128)(2,1)S(1)}, u32[]{:S(2)}, u32[]{:S(2)}) collective-permute-start(bf16[128,1792]{1,0:T(8,128)(2,1)} %get-tuple-element.23), channel_id=1, source_target_pairs={{0,16},{24,8},{1,17},{25,9},{2,18},{26,10},{3,19},{27,11},{4,20},{... | collective-permute-start | bytes 1376264 | tf_op jit(solution)/shard_map/ppermute | solution.py:714
  10.7 22.5 %collective-permute-start.4 = (bf16[128,1792]{1,0:T(8,128)(2,1)}, bf16[128,1792]{1,0:T(8,128)(2,1)S(1)}, u32[]{:S(2)}, u32[]{:S(2)}) collective-permute-start(bf16[128,1792]{1,0:T(8,128)(2,1)} %get-tuple-element.23), channel_id=1, source_target_pairs={{8,24},{16,0},{9,25},{17,1},{10,26},{18,2},{11,27},{19,3},{12,28},... | collective-permute-start | bytes 1376264 | tf_op jit(solution)/shard_map/ppermute | solution.py:714
  12.0 21.2 %collective-permute-start = (f32[40,128]{1,0:T(8,128)}, f32[40,128]{1,0:T(8,128)S(1)}, u32[]{:S(2)}, u32[]{:S(2)}) collective-permute-start(f32[40,128]{1,0:T(8,128)} %get-tuple-element.21), channel_id=1, source_target_pairs={{0,16},{1,17},{2,18},{3,19},{4,20},{5,21},{6,22},{7,23},{8,24},{9,... | collective-permute-start | bytes 61448 | tf_op jit(solution)/shard_map/ppermute | solution.py:701
  52.6 42.5 %all-to-all-start.2 = ((bf16[16,16,3584]{2,1,0:T(8,128)(2,1)}), bf16[16,16,3584]{2,1,0:T(8,128)(2,1)}, u32[]{:S(2)}, u32[]{:S(2)}) async-start(bf16[16,16,3584]{2,1,0:T(8,128)(2,1)} %bitcast.43), calls=%async_computation.2 | async-start | bytes 3670016 | tf_op jit(solution)/shard_map/all_to_all | solution.py:718
  57.0 36.1 %collective-permute-start.1 = (bf16[128,1792]{1,0:T(8,128)(2,1)S(1)}, bf16[128,1792]{1,0:T(8,128)(2,1)S(1)}, u32[]{:S(2)}, u32[]{:S(2)}) collective-permute-start(bf16[128,1792]{1,0:T(8,128)(2,1)S(1)} %copy-done.16), channel_id=1, source_target_pairs={{0,16},{24,8},{1,17},{25,9},{2,18},{26,10},{3,19},{27,11},{4,20},{... | collective-permute-start | bytes 1376264 | tf_op jit(solution)/shard_map/ppermute | solution.py:714
  61.5 31.7 %collective-permute-start.2 = (bf16[128,1792]{1,0:T(8,128)(2,1)S(1)}, bf16[128,1792]{1,0:T(8,128)(2,1)S(1)}, u32[]{:S(2)}, u32[]{:S(2)}) collective-permute-start(bf16[128,1792]{1,0:T(8,128)(2,1)S(1)} %copy-done.16), channel_id=1, source_target_pairs={{8,24},{16,0},{9,25},{17,1},{10,26},{18,2},{11,27},{19,3},{12,28},... | collective-permute-start | bytes 1376264 | tf_op jit(solution)/shard_map/ppermute | solution.py:714
  62.8 27.4 %collective-permute-start.5 = (f32[40,128]{1,0:T(8,128)S(1)}, f32[40,128]{1,0:T(8,128)S(1)}, u32[]{:S(2)}, u32[]{:S(2)}) collective-permute-start(f32[40,128]{1,0:T(8,128)S(1)} %copy-done.15), channel_id=1, source_target_pairs={{0,8},{1,9},{2,10},{3,11},{4,12},{5,13},{6,14},{7,15},{8,0},{9,1},... | collective-permute-start | bytes 61448 | tf_op jit(solution)/shard_map/ppermute | solution.py:701
  65.7 27.3 %collective-permute-start.6 = (f32[40,128]{1,0:T(8,128)S(1)}, f32[40,128]{1,0:T(8,128)S(1)}, u32[]{:S(2)}, u32[]{:S(2)}) collective-permute-start(f32[40,128]{1,0:T(8,128)S(1)} %copy-done.15), channel_id=1, source_target_pairs={{0,24},{1,25},{2,26},{3,27},{4,28},{5,29},{6,30},{7,31},{8,16},{9,... | collective-permute-start | bytes 61448 | tf_op jit(solution)/shard_map/ppermute | solution.py:701
  93.1 8.9 %collective-permute-start.7 = (f32[4,40,128]{2,1,0:T(8,128)S(1)}, f32[4,40,128]{2,1,0:T(8,128)S(1)}, u32[]{:S(2)}, u32[]{:S(2)}) collective-permute-start(f32[4,40,128]{2,1,0:T(8,128)S(1)} %pad_maximum_fusion), channel_id=1, source_target_pairs={{0,1},{1,0},{2,3},{3,2},{4,5},{5,4},{6,7},{7,6},{8,9},{9,8},{10,11... | collective-permute-start | bytes 245768 | tf_op jit(solution)/shard_map/ppermute | solution.py:707
  93.2 50.3 %slice-start = ((s8[7340032]{0:T(1024)(128)(4,1)}), s8[3145728]{0:T(1024)(128)(4,1)S(1)}, s32[]{:S(2)}) async-start(s8[7340032]{0:T(1024)(128)(4,1)} %bitcast.34), calls=%async_computation.4 | async-start | bytes 6291456
  94.1 1.0 copy-start.5
  95.1 54.3 %all-to-all-start = ((bf16[16,16,1792]{2,1,0:T(8,128)(2,1)}), bf16[16,16,1792]{2,1,0:T(8,128)(2,1)}, u32[]{:S(2)}, u32[]{:S(2)}) async-start(bf16[16,16,1792]{2,1,0:T(8,128)(2,1)} %bitcast.40), calls=%async_computation | async-start | bytes 1835008 | tf_op jit(solution)/shard_map/all_to_all | solution.py:718
  102.7 14.9 %collective-permute-start.8 = (f32[8,40,128]{2,1,0:T(8,128)S(1)}, f32[8,40,128]{2,1,0:T(8,128)S(1)}, u32[]{:S(2)}, u32[]{:S(2)}) collective-permute-start(f32[8,40,128]{2,1,0:T(8,128)S(1)} %get-tuple-element.43), channel_id=1, source_target_pairs={{0,2},{1,3},{2,0},{3,1},{4,6},{5,7},{6,4},{7,5},{8,10},{9,11},{10,... | collective-permute-start | bytes 491528 | tf_op jit(solution)/shard_map/ppermute | solution.py:707
  118.3 9.9 %collective-permute-start.9 = (f32[16,40,128]{2,1,0:T(8,128)}, f32[16,40,128]{2,1,0:T(8,128)S(1)}, u32[]{:S(2)}, u32[]{:S(2)}) collective-permute-start(f32[16,40,128]{2,1,0:T(8,128)} %get-tuple-element.39), channel_id=1, source_target_pairs={{0,4},{1,5},{2,6},{3,7},{4,0},{5,1},{6,2},{7,3},{8,12},{9,13},{10,... | collective-permute-start | bytes 983048 | tf_op jit(solution)/shard_map/ppermute | solution.py:707
  118.8 24.7 %copy-start.14 = (s32[2]{0:T(128)}, s32[2]{0:T(128)S(1)}, u32[]{:S(2)}) copy-start(s32[2]{0:T(128)S(1)} %pad_add_fusion.table_ref) | copy-start | bytes 28
  135.9 3.1 %copy-start = (bf16[1,1024,3584]{2,1,0:T(8,128)(2,1)S(1)}, bf16[1,1024,3584]{2,1,0:T(8,128)(2,1)}, u32[]{:S(2)}) copy-start(bf16[1,1024,3584]{2,1,0:T(8,128)(2,1)} %param.11) | copy-start | bytes 22020100
  139.0 1.2 copy-start.4
  140.2 3.3 %slice-start.1 = ((s8[7340032]{0:T(1024)(128)(4,1)}), s8[4194304]{0:T(1024)(128)(4,1)S(1)}, s32[]{:S(2)}) async-start(s8[7340032]{0:T(1024)(128)(4,1)} %bitcast.34), calls=%async_computation.5 | async-start | bytes 8388608
  140.2 3.3 %copy-start.2 = (bf16[1,512,1024]{2,1,0:T(8,128)(2,1)S(1)}, bf16[1,512,1024]{2,1,0:T(8,128)(2,1)}, u32[]{:S(2)}) copy-start(bf16[1,512,1024]{2,1,0:T(8,128)(2,1)} %param.10) | copy-start | bytes 3145732
  140.2 3.3 %copy-start.6 = (f32[512,128]{1,0:T(8,128)S(1)}, f32[512,128]{1,0:T(8,128)}, u32[]{:S(2)}) copy-start(f32[512,128]{1,0:T(8,128)} %get-tuple-element.24.refs_1_.refs_2_) | copy-start | bytes 786436
  142.5 1.0 copy-start.1
  148.8 0.6 copy-start.11
  149.4 15.7 %copy-start.3 = (f32[6,32,40,128]{3,2,1,0:T(8,128)S(1)}, f32[6,32,40,128]{3,2,1,0:T(8,128)}, u32[]{:S(2)}) copy-start(f32[6,32,40,128]{3,2,1,0:T(8,128)} %get-tuple-element.30.level_ref) | copy-start | bytes 11796484
  149.4 15.7 %copy-start.7 = (f32[5,32,8,128]{3,2,1,0:T(8,128)S(1)}, f32[5,32,8,128]{3,2,1,0:T(8,128)}, u32[]{:S(2)}) copy-start(f32[5,32,8,128]{3,2,1,0:T(8,128)} %get-tuple-element.31.inverse_ref) | copy-start | bytes 1966084
  149.4 15.7 %copy-start.8 = (f32[32,32,128]{2,1,0:T(8,128)S(1)}, f32[32,32,128]{2,1,0:T(8,128)}, u32[]{:S(2)}) copy-start(f32[32,32,128]{2,1,0:T(8,128)} %get-tuple-element.33.seed_q_ref) | copy-start | bytes 1572868
  149.4 15.7 %copy-start.9 = (f32[32,32,128]{2,1,0:T(8,128)S(1)}, f32[32,32,128]{2,1,0:T(8,128)}, u32[]{:S(2)}) copy-start(f32[32,32,128]{2,1,0:T(8,128)} %get-tuple-element.34.seed_p_ref) | copy-start | bytes 1572868
  149.4 15.7 %copy-start.10 = (s32[32,32,128]{2,1,0:T(8,128)S(1)}, s32[32,32,128]{2,1,0:T(8,128)}, u32[]{:S(2)}) copy-start(s32[32,32,128]{2,1,0:T(8,128)} %get-tuple-element.35.where_ref) | copy-start | bytes 1572868
  149.4 15.7 %copy-start.12 = (f32[5,40,128]{2,1,0:T(8,128)S(1)}, f32[5,40,128]{2,1,0:T(8,128)}, u32[]{:S(2)}) copy-start(f32[5,40,128]{2,1,0:T(8,128)} %get-tuple-element.32.column_ref) | copy-start | bytes 307204
  149.4 15.7 %copy-start.13 = (f32[40,128]{1,0:T(8,128)S(1)}, f32[40,128]{1,0:T(8,128)}, u32[]{:S(2)}) copy-start(f32[40,128]{1,0:T(8,128)} %get-tuple-element.36.own_ref) | copy-start | bytes 61444
